TPU v7x, 32 devices: a whole 2x2x4 slice. The times are simulated.
32 devices in a mesh: groups: 2 (over x), win: 4 (over y, core), rcv: 4 (over z).
Axes of the slice: x: 2, y: 2, z: 4, core: 2. Of those that a mesh axis runs over, the one named last changes fastest.
Arguments:
- traces: bfloat16 [32, 768, 4096], P('win', ('groups', 'rcv')), parts along dimension 1, may hold values from -6 to 6
- valid: int32 [64], P(('groups', 'win')), parts along dimension 0, may hold values 0 or 1
- src_station: int32 [64], P('groups'), parts along dimension 0, may hold values from 0 to 383, as said below
Outputs:
- stacks: float32 [32, 768, 2, 512], P(None, ('groups', 'rcv'), None, 'win'), parts along dimension 1
There are 2 independent parts, one for each index of `groups`. A program takes and returns all parts, laid end to end along the dimension named above; each array names one. Nothing has to cross between parts.
Inputs may be any that keep to these rules, and one draw needn't show every extreme that they name: `src_station`: distinct stations; station 0 and station 384 - 1 are always among them.
All inputs are finite; a program needn't handle non-finite values. No bound on the sum of `valid` on one device may be relied on, other than what follows from the above.
Results may differ from a plain program's by a relative error of at most 0.0049.
Values may be sent and summed in bfloat16 or wider, within the bound.
A program may use at most 128 MiB of HBM per device.

v0:
```python
import math

import jax
import jax.numpy as jnp
from jax import lax
from jax.sharding import PartitionSpec as P

F = 512


def band_table(count, bins, first):
    samples = jnp.arange(count, dtype=jnp.int32)
    freqs = first + jnp.arange(bins, dtype=jnp.int32)
    phase = samples[:, None] * freqs[None, :] % count
    angle = phase.astype(jnp.float32) * (2.0 * math.pi / count)
    return jnp.concatenate([jnp.cos(angle), -jnp.sin(angle)], axis=1).astype(jnp.bfloat16)


def correlate(received, sources):
    rr = received[:, :, 0]
    ri = received[:, :, 1]
    sr = sources[:, :, 0]
    si = sources[:, :, 1]
    real = jnp.einsum("wsf,wrf->srf", sr, rr, preferred_element_type=jnp.float32)
    real = real + jnp.einsum("wsf,wrf->srf", si, ri, preferred_element_type=jnp.float32)
    imag = jnp.einsum("wsf,wrf->srf", sr, ri, preferred_element_type=jnp.float32)
    imag = imag - jnp.einsum("wsf,wrf->srf", si, rr, preferred_element_type=jnp.float32)
    return jnp.stack([real, imag], axis=2)


def body(traces, valid, src_station):
    w_dev, r_dev, samples = traces.shape
    bins = F
    table = band_table(samples, bins, samples // 16)
    spectra = jnp.dot(
        traces.reshape(w_dev * r_dev, samples), table, preferred_element_type=jnp.float32
    )
    spectra = spectra.reshape(w_dev, r_dev, 2, bins)
    power = jnp.sum(spectra * spectra, axis=(2, 3), keepdims=True) / bins
    white = (spectra * lax.rsqrt(power + 1e-06)).astype(jnp.bfloat16)
    received = white * valid.astype(jnp.bfloat16)[:, None, None, None]
    offset = lax.axis_index("rcv") * r_dev
    station_ids = offset + jnp.arange(r_dev, dtype=jnp.int32)
    selector = (src_station[:, None] == station_ids[None, :]).astype(jnp.bfloat16)
    local_rows = jnp.einsum("sr,wrcf->wscf", selector, white, preferred_element_type=jnp.float32)
    sources = lax.psum(local_rows.astype(jnp.bfloat16), "rcv")
    scale = 1.0 / math.sqrt(w_dev * lax.axis_size("win"))
    partial_stacks = correlate(received, sources)
    stacks = lax.psum_scatter(partial_stacks, "win", scatter_dimension=3, tiled=True)
    return stacks * scale


def solution(mesh):
    return jax.shard_map(
        body,
        mesh=mesh,
        in_specs=(P("win", ("groups", "rcv"), None), P(("groups", "win")), P("groups")),
        out_specs=P(None, ("groups", "rcv"), None, "win"),
        check_vma=False,
    )
```

profile of v0, /device:TPU:0, one launch (start us, length us, event | category | flops | bytes accessed | tf_op | source)
XLA Modules:
  0.0 262.6 jit_solution(9068600715958366044)
XLA Ops:
  6.5 0.7 convert_element_type.21
  7.2 34.0 %cosine_convert_fusion = (bf16[4096,512]{1,0:T(8,128)(2,1)S(1)}, bf16[4096,512]{1,0:T(8,128)(2,1)S(1)}) fusion(s32[512]{0:T(512)S(1)} %iota_add_fusion), kind=kLoop, calls=%fused_computation.15 | loop fusion | flops 35651584 | bytes 8390656 | tf_op jit(solution)/shard_map/convert
  41.2 9.5 %multiply_reduce_fusion = (f32[768]{0:T(1024)S(1)}, f32[768,1024]{0,1:T(8,128)S(1)}) fusion(bf16[768,4096]{1,0:T(8,128)(2,1)} %bitcast.45, bf16[4096,512]{1,0:T(8,128)(2,1)S(1)} %get-tuple-element.10, bf16[4096,512]{1,0:T(8,128)(2,1)S(1)} %get-tuple-element.9), kind=kOutput, calls=%fused_computation.20 | convolution fusion | flops 6460800000 | bytes 17828864 | tf_op jit(solution)/shard_map/dot_general | solution.py:35
  50.7 0.1 rsqrt.12
  50.8 3.1 %reshape.36 = f32[8,96,2,512]{1,0,3,2:T(8,128)} reshape(f32[768,1024]{0,1:T(8,128)S(1)} %get-tuple-element.12) | data formatting | bytes 6291456 | tf_op jit(solution)/shard_map/reshape | solution.py:38
  53.9 2.9 %broadcast_multiply_fusion.1 = (bf16[8,96,2,512]{1,0,3,2:T(8,128)(2,1)S(1)}, bf16[8,96,2,512]{1,0,3,2:T(8,128)(2,1)S(1)}) fusion(bf16[8]{0:T(256)(128)(2,1)S(1)} %convert_element_type.21, f32[8,96,2,512]{1,0,3,2:T(8,128)} %reshape.36, f32[8,96]{1,0:T(8,128)S(1)} %rsqrt.12), kind=kLoop, calls=%fused_computation.29 | loop fusion | flops 2359296 | bytes 6294544 | tf_op jit(solution)/shard_map/mul | solution.py:41
  56.8 1.6 fusion.18
  58.5 0.2 reduce-scatter.4.cloned.1.call-start
  58.7 40.9 %all-reduce.2.cloned.1.call-done = bf16[8,32,2,512]{3,1,2,0:T(8,128)(2,1)} async-done(((bf16[8,32,2,512]{3,1,2,0:T(8,128)(2,1)}), bf16[8,32,2,512]{3,1,2,0:T(8,128)(2,1)}) %all-reduce.2.cloned.1.call-update) | async-done | bytes 524304 | tf_op jit(solution)/shard_map/psum | solution.py:46
  99.7 1.8 slice_bitcast_fusion.6
  101.4 1.7 copy.29
  103.2 4.0 %fusion.22 = f32[512,96,32]{1,2,0:T(8,128)} fusion(bf16[8,32,512]{1,0,2:T(8,128)(2,1)S(1)} %copy.29, bf16[8,96,2,512]{1,0,3,2:T(8,128)(2,1)S(1)} %get-tuple-element.5), kind=kOutput, calls=%fused_computation.31 | convolution fusion | flops 25165824 | bytes 8388608 | tf_op jit(solution)/shard_map/wsf,wrf->srf/dot_general | solution.py:26
  107.2 4.0 %fusion.21 = f32[512,96,32]{1,2,0:T(8,128)} fusion(bf16[8,32,512]{1,0,2:T(8,128)(2,1)S(1)} %copy.29, bf16[8,96,2,512]{1,0,3,2:T(8,128)(2,1)S(1)} %get-tuple-element.5), kind=kOutput, calls=%fused_computation.30 | convolution fusion | flops 25165824 | bytes 8388608 | tf_op jit(solution)/shard_map/wsf,wrf->srf/dot_general | solution.py:24
  111.2 0.8 copy.30
  111.9 4.4 %subtract_bitcast_fusion = f32[32,96,1,512]{1,0,3,2:T(8,128)S(1)} fusion(f32[512,96,32]{1,2,0:T(8,128)} %fusion.22, bf16[8,32,512]{1,0,2:T(8,128)(2,1)S(1)} %copy.30, bf16[8,96,2,512]{1,0,3,2:T(8,128)(2,1)S(1)} %get-tuple-element.5), kind=kOutput, calls=%fused_computation.12 | convolution fusion | flops 26738688 | bytes 14680064 | tf_op jit(solution)/shard_map/wsf,wrf->srf/dot_general | solution.py:27
  116.3 1.4 copy-done
  117.8 1.3 add_bitcast_fusion
  119.1 6.3 %copy_bitcast_fusion = f32[512,2,32,96]{3,2,1,0:T(8,128)} fusion(f32[32,96,1,512]{1,0,3,2:T(8,128)S(1)} %subtract_bitcast_fusion, f32[32,96,1,512]{1,0,3,2:T(8,128)S(1)} %add_bitcast_fusion), kind=kLoop, calls=%fused_computation.1 | loop fusion | flops 3145728 | bytes 25165824
  125.4 17.7 %reshape.37 = f32[512,6144]{1,0:T(8,128)} reshape(f32[512,2,32,96]{3,2,1,0:T(8,128)} %copy_bitcast_fusion) | data formatting | bytes 25165824
  143.1 99.2 %reduce-scatter.4.cloned.1.call-done = f32[128,6144]{1,0:T(8,128)} async-done(((f32[512,6144]{1,0:T(8,128)}), f32[128,6144]{1,0:T(8,128)}) %reduce-scatter.4.cloned.1.call-update) | async-done | bytes 3145744
  242.3 5.4 %reshape.38 = f32[128,2,32,96]{3,2,1,0:T(8,128)} reshape(f32[128,6144]{1,0:T(8,128)} %reduce-scatter.4.cloned.1.call-done) | data formatting | bytes 6291456
  247.6 3.7 %copy.33 = f32[32,96,2,128]{3,1,2,0:T(8,128)S(1)} copy(f32[32,96,2,128]{1,0,2,3:T(8,128)} %bitcast.44) | data formatting | bytes 6291456 | tf_op jit(solution)/shard_map/reduce_scatter | solution.py:49
  251.4 0.3 broadcast_multiply_fusion
  251.7 4.1 %copy.34 = f32[32,96,2,128]{3,2,1,0:T(2,128)} copy(f32[32,96,2,128]{3,1,2,0:T(8,128)S(1)} %broadcast_multiply_fusion) | data formatting | bytes 6291456 | tf_op jit(solution)/shard_map/mul | solution.py:50
  (9 shorter events, 0.1 us)
Async XLA Ops:
  6.5 93.1 %all-reduce.2.cloned.1.call-start = ((), (), s32[]{:S(2)}) async-start(), calls=%async_computation.1 | async-start | bytes 1048576 | tf_op jit(solution)/shard_map/psum | solution.py:46
  50.7 6.1 %copy-start.1 = (s32[32]{0:T(128)S(1)}, s32[32]{0:T(128)}, u32[]{:S(2)}) copy-start(s32[32]{0:T(128)} %param.5) | copy-start | bytes 388
  58.5 183.8 %reduce-scatter.4.cloned.1.call-start = ((), (), s32[]{:S(2)}) async-start(), calls=%async_computation.2 | async-start | bytes 15728640
  111.9 5.8 %copy-start = (f32[512,96,32]{1,2,0:T(8,128)S(1)}, f32[512,96,32]{1,2,0:T(8,128)}, u32[]{:S(2)}) copy-start(f32[512,96,32]{1,2,0:T(8,128)} %fusion.21) | copy-start | bytes 18874372
Sparse Core Ops, SparseCore 0:
  58.6 40.9 all-reduce.1
  143.2 99.0 reduce-scatter.3
where the time goes:
time: 263 us
  waiting for transfers between devices  140 us (53%)
  other arithmetic  44.1 us (17%)
  local copies, waits for them, and re-layouts  39.8 us (15%)
  matrix products  24.8 us (9%)
  between operations  13.5 us (5%)
    unnamed x3, waiting for transfers between devices  99.2 us
    psum x1, waiting for transfers between devices, body(): sources = lax.psum(local_rows.astype(jnp.bfloat16), 'rcv')  40.9 us
    another operation x1, other arithmetic  34 us
    unnamed x6, local copies, waits for them, and re-layouts  24.5 us
    dot_general x1, matrix products, body(): jnp.dot(traces.reshape(w_dev * r_dev, samples), table, preferred_element_...  9.49 us
    unnamed x1, other arithmetic  6.25 us
  transfers between devices with their start and end apart: 2, of which 2 were waited for; matrix products, arithmetic and copies ran while one was open for 0% of the time, Pallas kernels for 0%

commit v1 on v0

v1 whole, which is shorter than its diff:
```python
import math

import jax
import jax.numpy as jnp
import ml_dtypes
import numpy as np
from jax import lax
from jax.sharding import PartitionSpec as P

F = 512


def band_table(count, bins, first):
    samples = np.arange(count, dtype=np.int64)
    freqs = first + np.arange(bins, dtype=np.int64)
    phase = samples[:, None] * freqs[None, :] % count
    angle = phase.astype(np.float64) * (2.0 * math.pi / count)
    return np.concatenate([np.cos(angle), -np.sin(angle)], axis=1).astype(ml_dtypes.bfloat16)


def body(traces, valid, src_station):
    w_dev, r_dev, samples = traces.shape
    bins = F
    n_win = lax.axis_size("win")
    f_dev = bins // n_win
    table = jnp.asarray(band_table(samples, bins, samples // 16))
    spectra = jnp.dot(
        traces.reshape(w_dev * r_dev, samples), table, preferred_element_type=jnp.float32
    )
    power = jnp.sum(spectra * spectra, axis=1, keepdims=True) / bins
    keep = jnp.repeat(valid.astype(jnp.float32), r_dev)[:, None]
    white = (spectra * (lax.rsqrt(power + 1e-06) * keep)).astype(jnp.bfloat16)
    white = white.reshape(w_dev * r_dev, 2, n_win, f_dev)
    pieces = jnp.transpose(white, (2, 1, 0, 3))
    got = lax.all_to_all(pieces, "win", 0, 0, tiled=True)
    got = got.reshape(n_win, 2, w_dev, r_dev, f_dev)
    offset = lax.axis_index("rcv") * r_dev
    station_ids = offset + jnp.arange(r_dev, dtype=jnp.int32)
    selector = (src_station[:, None] == station_ids[None, :]).astype(jnp.bfloat16)
    rows = jnp.einsum("sr,gcwrf->gcwsf", selector, got, preferred_element_type=jnp.float32)
    src = lax.psum(rows.astype(jnp.bfloat16), "rcv")
    scale = 1.0 / math.sqrt(w_dev * n_win)
    turned = jnp.stack([got[:, 1], -got[:, 0]], axis=1)
    real = jnp.einsum("gcwsf,gcwrf->srf", src, got, preferred_element_type=jnp.float32)
    imag = jnp.einsum("gcwsf,gcwrf->srf", src, turned, preferred_element_type=jnp.float32)
    return jnp.stack([real, imag], axis=2) * scale


def solution(mesh):
    return jax.shard_map(
        body,
        mesh=mesh,
        in_specs=(P("win", ("groups", "rcv"), None), P(("groups", "win")), P("groups")),
        out_specs=P(None, ("groups", "rcv"), None, "win"),
        check_vma=False,
    )
```

time: 263 us -> 114 us (0.43)
  waiting for transfers between devices: 140 us -> 53.4 us
  other arithmetic: 44.1 us -> 1.54 us
  local copies, waits for them, and re-layouts: 39.8 us -> 21.2 us
  matrix products: 24.8 us -> 19.5 us
  starting transfers between devices: 0.22 us -> 4.24 us
    unnamed x3 -> x1, waiting for transfers between devices: 99.2 us -> 0.02 us
    another operation x1, other arithmetic: 34 us -> 0.15 us  [body(): turned = jnp.stack([got[:, 1], -got[:, 0]], axis=1)]
    unnamed x6 -> x4, local copies, waits for them, and re-layouts: 24.5 us -> 0.01 us
    all_to_all x0 -> x1, waiting for transfers between devices: none -> 20.1 us  [body(): got = lax.all_to_all(pieces, 'win', 0, 0, tiled=True)]
    psum x1, waiting for transfers between devices: 40.9 us -> 33.3 us  [body(): src = lax.psum(rows.astype(jnp.bfloat16), 'rcv')]
    dot_general x5 -> x3, matrix products: 15.3 us -> 8.49 us  [the longest x1 3.65 us: body(): jnp.einsum('gcwsf,gcwrf->srf', src, got, preferred_element_type=jnp.float32)]
    unnamed x1 -> x0, other arithmetic: 6.25 us -> none
    dot_general x0 -> x2, local copies, waits for them, and re-layouts: none -> 5.11 us  [the longest x1 2.94 us: body(): jnp.einsum('gcwsf,gcwrf->srf', src, turned, preferred_element_type=jnp.fl...]
  transfers between devices with their start and end apart: 2 -> 2, of which waited for: 2 -> 2; matrix products, arithmetic and copies ran while one was open for 0% -> 5% of each run, Pallas kernels for 0% -> 0%
where the time goes in v1:
time: 114 us; the launch traced here: 113 us
  waiting for transfers between devices  53.4 us (47%)
  local copies, waits for them, and re-layouts  21.2 us (19%)
  matrix products  19.5 us (17%)
  between operations  13.5 us (12%)
  starting transfers between devices  4.24 us (4%)
  other arithmetic  1.54 us (1%)
    psum x1, waiting for transfers between devices, body(): src = lax.psum(rows.astype(jnp.bfloat16), 'rcv')  33.3 us
    all_to_all x1, waiting for transfers between devices, body(): got = lax.all_to_all(pieces, 'win', 0, 0, tiled=True)  20.1 us
    dot_general x1, matrix products, body(): jnp.dot(traces.reshape(w_dev * r_dev, samples), table, preferred_element_...  11 us
    all_to_all x1, starting transfers between devices, body(): got = lax.all_to_all(pieces, 'win', 0, 0, tiled=True)  4.24 us
    mul x1, local copies, waits for them, and re-layouts, body(): return jnp.stack([real, imag], axis=2) * scale  4.1 us
    psum x1, local copies, waits for them, and re-layouts, body(): src = lax.psum(rows.astype(jnp.bfloat16), 'rcv')  3.88 us
    dot_general x1, matrix products, body(): jnp.einsum('gcwsf,gcwrf->srf', src, got, preferred_element_type=jnp.float32)  3.65 us
    dot_general x1, matrix products, body(): jnp.einsum('gcwsf,gcwrf->srf', src, turned, preferred_element_type=jnp.fl...  3.64 us
  transfers between devices with their start and end apart: 2, of which 2 were waited for; matrix products, arithmetic and copies ran while one was open for 5% of the time, Pallas kernels for 0%

profile of v1, /device:TPU:0, one launch (start us, length us, event | category | flops | bytes accessed | tf_op | source)
XLA Modules:
  0.0 113.4 jit_solution(5430483913655910019)
XLA Ops:
  6.5 0.7 convert_element_type.13
  7.2 0.1 broadcast_in_dim.2
  7.3 0.1 broadcast_in_dim_reshape.3
  7.3 11.0 %multiply_reduce_fusion = (f32[768]{0:T(1024)S(1)}, f32[1024,768]{1,0:T(8,128)S(1)}) fusion(bf16[4096,1024]{1,0:T(8,128)(2,1)} %constant.17.clone, bf16[768,4096]{1,0:T(8,128)(2,1)} %bitcast.42), kind=kOutput, calls=%fused_computation.2 | convolution fusion | flops 6444022784 | bytes 17828864 | tf_op jit(solution)/shard_map/dot_general | solution.py:27
  18.4 0.3 multiply_convert_fusion
  18.7 1.3 %copy.31 = bf16[768,2,4,128]{0,3,1,2:T(8,128)(2,1)} copy(bf16[768,2,4,128]{0,3,2,1:T(8,128)(2,1)S(1)} %bitcast.41) | data formatting | bytes 3145728 | tf_op jit(solution)/shard_map/reshape | solution.py:33
  19.9 4.2 %all-to-all-start = ((bf16[4,2,768,128]{2,3,1,0:T(8,128)(2,1)}), bf16[4,2,768,128]{2,3,1,0:T(8,128)(2,1)S(1)}, u32[]{:S(2)}, u32[]{:S(2)}) async-start(bf16[4,2,768,128]{2,3,1,0:T(8,128)(2,1)} %bitcast.35), calls=%async_computation | async-start | bytes 3145728 | tf_op jit(solution)/shard_map/all_to_all | solution.py:35
  24.2 0.0 all-reduce.2.cloned.1.call-start
  24.2 20.1 %all-to-all-done = bf16[4,2,768,128]{2,3,1,0:T(8,128)(2,1)S(1)} async-done(((bf16[4,2,768,128]{2,3,1,0:T(8,128)(2,1)}), bf16[4,2,768,128]{2,3,1,0:T(8,128)(2,1)S(1)}, u32[]{:S(2)}, u32[]{:S(2)}) %all-to-all-start) | async-done | bytes 1572896 | tf_op jit(solution)/shard_map/all_to_all | solution.py:35
  44.2 0.9 copy.19
  45.2 1.2 %fusion = bf16[4,2,8,32,128]{4,3,2,1,0:T(8,128)(2,1)} fusion(bf16[4,2,8,96,128]{4,3,2,1,0:T(8,128)(2,1)S(1)} %bitcast.36, s32[96]{0:T(128)S(1)} %iota_add_fusion, s32[32]{0:T(128)S(1)} %copy-done.1), kind=kOutput, calls=%fused_computation.8 | convolution fusion | flops 50596864 | bytes 2097664 | tf_op jit(solution)/shard_map/sr,gcwrf->gcwsf/dot_general | solution.py:40
  46.4 0.0 all-reduce.2.cloned.1.call-update
  46.4 3.0 %copy.20 = bf16[4,2,8,96,128]{3,2,0,1,4:T(8,128)(2,1)} copy(bf16[4,2,8,96,128]{4,3,2,1,0:T(8,128)(2,1)S(1)} %bitcast.37) | data formatting | bytes 3145728 | tf_op jit(solution)/shard_map/reshape | solution.py:36
  49.4 0.2 fusion.5
  49.5 0.1 pad_maximum_fusion
  49.7 2.9 %copy.23 = bf16[4,2,8,96,128]{3,2,0,1,4:T(8,128)(2,1)} copy(bf16[4,2,8,96,128]{4,3,2,1,0:T(8,128)(2,1)S(1)} %pad_maximum_fusion) | data formatting | bytes 3145728 | tf_op jit(solution)/shard_map/stack | solution.py:43
  52.6 33.3 %all-reduce.2.cloned.1.call-done = bf16[4,2,8,32,128]{4,3,2,1,0:T(8,128)(2,1)} async-done(((bf16[4,2,8,32,128]{4,3,2,1,0:T(8,128)(2,1)}), bf16[4,2,8,32,128]{4,3,2,1,0:T(8,128)(2,1)}) %all-reduce.2.cloned.1.call-update) | async-done | bytes 524304 | tf_op jit(solution)/shard_map/psum | solution.py:41
  85.8 3.9 %copy.21 = bf16[4,2,8,32,128]{3,2,0,1,4:T(8,128)(2,1)S(1)} copy(bf16[4,2,8,32,128]{4,3,2,1,0:T(8,128)(2,1)} %all-reduce.2.cloned.1.call-done) | data formatting | bytes 1048576 | tf_op jit(solution)/shard_map/psum | solution.py:41
  89.7 3.6 %convolution_bitcast_fusion = f32[128,96,32]{1,2,0:T(8,128)} fusion(bf16[4,2,8,96,128]{3,2,0,1,4:T(8,128)(2,1)} %copy.23, bf16[4,2,8,32,128]{3,2,0,1,4:T(8,128)(2,1)S(1)} %copy.21), kind=kOutput, calls=%fused_computation.3 | convolution fusion | flops 50331648 | bytes 3670016 | tf_op jit(solution)/shard_map/gcwsf,gcwrf->srf/dot_general | solution.py:45
  93.4 2.9 %copy.25 = f32[128,96,32]{0,1,2:T(8,128)} copy(f32[128,96,32]{1,2,0:T(8,128)} %convolution_bitcast_fusion) | data formatting | bytes 3145728 | tf_op jit(solution)/shard_map/gcwsf,gcwrf->srf/dot_general | solution.py:45
  96.3 3.6 %convolution_bitcast_fusion.1 = f32[128,96,32]{1,2,0:T(8,128)} fusion(bf16[4,2,8,96,128]{3,2,0,1,4:T(8,128)(2,1)} %copy.20, bf16[4,2,8,32,128]{3,2,0,1,4:T(8,128)(2,1)S(1)} %copy.21), kind=kOutput, calls=%fused_computation.4 | convolution fusion | flops 50331648 | bytes 3670016 | tf_op jit(solution)/shard_map/gcwsf,gcwrf->srf/dot_general | solution.py:44
  100.0 2.2 %copy.22 = f32[128,96,32]{0,1,2:T(8,128)S(1)} copy(f32[128,96,32]{1,2,0:T(8,128)} %convolution_bitcast_fusion.1) | data formatting | bytes 3145728 | tf_op jit(solution)/shard_map/gcwsf,gcwrf->srf/dot_general | solution.py:44
  102.1 0.3 maximum_multiply_fusion
  102.5 4.1 %copy.26 = f32[32,96,2,128]{3,2,1,0:T(2,128)} copy(f32[32,96,2,128]{3,1,2,0:T(8,128)S(1)} %maximum_multiply_fusion) | data formatting | bytes 6291456 | tf_op jit(solution)/shard_map/mul | solution.py:46
  (6 shorter events, 0.0 us)
Async XLA Ops:
  19.9 24.3 %all-to-all-start = ((bf16[4,2,768,128]{2,3,1,0:T(8,128)(2,1)}), bf16[4,2,768,128]{2,3,1,0:T(8,128)(2,1)S(1)}, u32[]{:S(2)}, u32[]{:S(2)}) async-start(bf16[4,2,768,128]{2,3,1,0:T(8,128)(2,1)} %bitcast.35), calls=%async_computation | async-start | bytes 3145728 | tf_op jit(solution)/shard_map/all_to_all | solution.py:35
  24.2 21.0 %copy-start.1 = (s32[32]{0:T(128)S(1)}, s32[32]{0:T(128)}, u32[]{:S(2)}) copy-start(s32[32]{0:T(128)} %param.6) | copy-start | bytes 388
  24.2 61.7 %all-reduce.2.cloned.1.call-start = ((), (), s32[]{:S(2)}) async-start(), calls=%async_computation.1 | async-start | bytes 1048576 | tf_op jit(solution)/shard_map/psum | solution.py:41
  100.0 2.2 %copy-start = (f32[128,96,32]{0,1,2:T(8,128)S(1)}, f32[128,96,32]{0,1,2:T(8,128)}, u32[]{:S(2)}) copy-start(f32[128,96,32]{0,1,2:T(8,128)} %copy.25) | copy-start | bytes 4718596
Sparse Core Ops, SparseCore 0:
  46.5 39.2 all-reduce.1

commit v2 on v1

--- a/solution.py
+++ b/solution.py
@@ -1,3 +1,4 @@
+import functools
 import math
 
 import jax
@@ -5,9 +6,14 @@
 import ml_dtypes
 import numpy as np
 from jax import lax
+from jax.experimental import pallas as pl
+from jax.experimental.pallas import tpu as pltpu
 from jax.sharding import PartitionSpec as P
 
 F = 512
+SPLIT = 64
+MM = 2
+MESH = pl.DeviceIdType.MESH
 
 
 def band_table(count, bins, first):
@@ -18,7 +24,18 @@
     return np.concatenate([np.cos(angle), -np.sin(angle)], axis=1).astype(ml_dtypes.bfloat16)
 
 
-def body(traces, valid, src_station):
+def angle_factors(count, bins, first):
+    freqs = first + np.arange(bins, dtype=np.int64)
+    coarse = np.arange(count // SPLIT, dtype=np.int64)[:, None] * SPLIT * freqs[None, :] % count
+    fine = np.arange(SPLIT, dtype=np.int64)[:, None] * freqs[None, :] % count
+    out = []
+    for phase in (coarse, fine):
+        angle = phase.astype(np.float64) * (2.0 * math.pi / count)
+        out += [np.cos(angle).astype(np.float32), np.sin(angle).astype(np.float32)]
+    return out
+
+
+def plain_body(traces, valid, src_station):
     w_dev, r_dev, samples = traces.shape
     bins = F
     n_win = lax.axis_size("win")
@@ -46,6 +63,233 @@
     return jnp.stack([real, imag], axis=2) * scale
 
 
+def kernel(
+    nw, nz, w_dev, r_dev, bins,
+    traces, c1, s1, c0, s0, keep, sel, out,
+    tr, table, spec, snd, got, own, pin, sin, pout, sout, srcf, rf,
+    tsem, ysend, yrecv, psend, precv, ssend, srecv,
+):
+    me = lax.axis_index("win")
+    z = lax.axis_index("rcv")
+    f_dev = bins // nw
+    peers = [lax.rem(me + d, nw) for d in range(1, nw)]
+    senders = [lax.rem(me + nw - d, nw) for d in range(1, nw)]
+    barrier = pltpu.get_barrier_semaphore()
+
+    def load(w):
+        return pltpu.make_async_copy(traces.at[w], tr.at[w], tsem.at[w])
+
+    for w in range(w_dev):
+        load(w).start()
+    for peer in peers:
+        pl.semaphore_signal(barrier, inc=1, device_id={"win": peer}, device_id_type=MESH)
+
+    @pl.when(z > 0)
+    def _():
+        pl.semaphore_signal(barrier, inc=1, device_id={"rcv": z - 1}, device_id_type=MESH)
+
+    @pl.when(z < nz - 1)
+    def _():
+        pl.semaphore_signal(barrier, inc=1, device_id={"rcv": z + 1}, device_id_type=MESH)
+
+    @pl.when(z == 0)
+    def _():
+        pin[...] = jnp.zeros_like(pin)
+
+    @pl.when(z == nz - 1)
+    def _():
+        sin[...] = jnp.zeros_like(sin)
+
+    def build(a, _):
+        ca, sa = c1[pl.ds(a, 1), :], s1[pl.ds(a, 1), :]
+        rows = pl.ds(pl.multiple_of(a * SPLIT, SPLIT), SPLIT)
+        table[rows, 0:bins] = (ca * c0[...] - sa * s0[...]).astype(jnp.bfloat16)
+        table[rows, bins:] = (-(sa * c0[...] + ca * s0[...])).astype(jnp.bfloat16)
+        return 0
+
+    lax.fori_loop(0, c1.shape[0], build, 0)
+    out[...] = jnp.zeros_like(out)
+
+    @pl.when((z > 0) & (z < nz - 1))
+    def _():
+        pl.semaphore_wait(barrier, nw + 1)
+
+    @pl.when((z == 0) | (z == nz - 1))
+    def _():
+        pl.semaphore_wait(barrier, nw)
+
+    def y_copy(k, w):
+        return pltpu.make_async_remote_copy(
+            src_ref=snd.at[peers[k], w], dst_ref=got.at[me, w],
+            send_sem=ysend.at[k, w], recv_sem=yrecv.at[k, w],
+            device_id={"win": peers[k]}, device_id_type=MESH,
+        )
+
+    def y_arrival(k, w):
+        return pltpu.make_async_remote_copy(
+            src_ref=snd.at[peers[k], w], dst_ref=got.at[senders[k], w],
+            send_sem=ysend.at[k, w], recv_sem=yrecv.at[k, w],
+            device_id={"win": peers[k]}, device_id_type=MESH,
+        )
+
+    def transform(t, _):
+        for wl in range(MM):
+            load(t * MM + wl).wait()
+        x = tr[pl.ds(t * MM, MM)].reshape(MM * r_dev, tr.shape[2])
+        for nb in range(2 * bins // 256):
+            cols = slice(nb * 256, nb * 256 + 256)
+            spec[:, cols] = jnp.dot(x, table[:, cols], preferred_element_type=jnp.float32)
+        for wl in range(MM):
+            w = t * MM + wl
+            rows = slice(wl * r_dev, (wl + 1) * r_dev)
+            s = spec[rows, :]
+            power = jnp.sum(s * s, axis=1, keepdims=True) / bins
+            gain = lax.rsqrt(power + 1e-06) * keep[w][:, 0:1]
+            for d in range(nw):
+                for c in range(2):
+                    lo = c * bins + d * f_dev
+                    snd[d, w, c] = (spec[rows, lo:lo + f_dev] * gain).astype(jnp.bfloat16)
+            for k in range(nw - 1):
+                y_copy(k, w).start()
+            got[me, w] = snd[me, w]
+        return 0
+
+    lax.fori_loop(0, w_dev // MM, transform, 0)
+
+    def right(j):
+        return pltpu.make_async_remote_copy(
+            src_ref=pout.at[j], dst_ref=pin.at[j], send_sem=psend.at[j], recv_sem=precv.at[j],
+            device_id={"rcv": lax.rem(z + 1, nz)}, device_id_type=MESH,
+        )
+
+    def left(j):
+        return pltpu.make_async_remote_copy(
+            src_ref=sout.at[j], dst_ref=sin.at[j], send_sem=ssend.at[j], recv_sem=srecv.at[j],
+            device_id={"rcv": lax.rem(z + nz - 1, nz)}, device_id_type=MESH,
+        )
+
+    def step(it, _):
+        @pl.when(it < w_dev)
+        def _():
+            for k in range(nw - 1):
+                y_arrival(k, it).wait_recv()
+            for g in range(nw):
+                for c in range(2):
+                    own[it, g, c] = jnp.dot(
+                        sel[...], got[g, it, c], preferred_element_type=jnp.float32
+                    ).astype(jnp.bfloat16)
+
+        jr = it - z
+
+        @pl.when((jr >= 0) & (jr < w_dev))
+        def _():
+            @pl.when(z > 0)
+            def _():
+                right(jr).wait_recv()
+
+            @pl.when(z < nz - 1)
+            def _():
+                pout[jr] = own[jr] + pin[jr]
+                right(jr).start()
+
+        jl = it - (nz - 1 - z)
+
+        @pl.when((jl >= 0) & (jl < w_dev))
+        def _():
+            @pl.when(z < nz - 1)
+            def _():
+                left(jl).wait_recv()
+
+            @pl.when(z > 0)
+            def _():
+                sout[jl] = own[jl] + sin[jl]
+                left(jl).start()
+
+        jc = it - (nz - 1)
+
+        @pl.when(jc >= 0)
+        def _():
+            srcf[...] = (own[jc] + pin[jc] + sin[jc]).astype(jnp.float32)
+            for g in range(nw):
+                re = got[g, jc, 0].astype(jnp.float32)
+                im = got[g, jc, 1].astype(jnp.float32)
+                rf[g, 0, pl.ds(0, r_dev, stride=2), :] = re
+                rf[g, 0, pl.ds(1, r_dev, stride=2), :] = im
+                rf[g, 1, pl.ds(0, r_dev, stride=2), :] = im
+                rf[g, 1, pl.ds(1, r_dev, stride=2), :] = -re
+
+            def accumulate(s, _):
+                total = out[s]
+                for g in range(nw):
+                    total = total + srcf[g, 0, pl.ds(s, 1), :] * rf[g, 0]
+                    total = total + srcf[g, 1, pl.ds(s, 1), :] * rf[g, 1]
+                out[s] = total
+                return 0
+
+            lax.fori_loop(0, out.shape[0], accumulate, 0)
+
+        return 0
+
+    lax.fori_loop(0, w_dev + nz - 1, step, 0)
+
+    def drain(w, _):
+        for k in range(nw - 1):
+            y_copy(k, w).wait_send()
+
+        @pl.when(z < nz - 1)
+        def _():
+            right(w).wait_send()
+
+        @pl.when(z > 0)
+        def _():
+            left(w).wait_send()
+
+        return 0
+
+    lax.fori_loop(0, w_dev, drain, 0)
+
+
+def body(traces, valid, src_station):
+    w_dev, r_dev, samples = traces.shape
+    nw, nz = lax.axis_size("win"), lax.axis_size("rcv")
+    f_dev = F // nw
+    n_src = src_station.shape[0]
+    if f_dev % 128 or r_dev % 16 or w_dev % MM:
+        return plain_body(traces, valid, src_station)
+    factors = [jnp.asarray(f) for f in angle_factors(samples, F, samples // 16)]
+    station_ids = lax.axis_index("rcv") * r_dev + jnp.arange(r_dev, dtype=jnp.int32)
+    sel = (src_station[:, None] == station_ids[None, :]).astype(jnp.bfloat16)
+    keep = jnp.broadcast_to(valid.astype(jnp.float32)[:, None, None], (w_dev, 1, 128))
+    vmem = pl.BlockSpec(memory_space=pltpu.VMEM)
+    bf16, f32 = jnp.bfloat16, jnp.float32
+    spectra = (nw, w_dev, 2, r_dev, f_dev)
+    rows = (w_dev, nw, 2, n_src, f_dev)
+    dma = pltpu.SemaphoreType.DMA
+    stacks = pl.pallas_call(
+        functools.partial(kernel, nw, nz, w_dev, r_dev, F),
+        out_shape=jax.ShapeDtypeStruct((n_src, 2 * r_dev, f_dev), f32),
+        in_specs=[pl.BlockSpec(memory_space=pl.ANY)] + [vmem] * 6,
+        out_specs=vmem,
+        scratch_shapes=[
+            pltpu.VMEM((w_dev, r_dev, samples), bf16),
+            pltpu.VMEM((samples, 2 * F), bf16),
+            pltpu.VMEM((MM * r_dev, 2 * F), f32),
+            pltpu.VMEM(spectra, bf16),
+            pltpu.VMEM(spectra, bf16),
+        ] + [pltpu.VMEM(rows, bf16)] * 5 + [
+            pltpu.VMEM((nw, 2, n_src, f_dev), f32),
+            pltpu.VMEM((nw, 2, 2 * r_dev, f_dev), f32),
+            dma((w_dev,)), dma((nw - 1, w_dev)), dma((nw - 1, w_dev)),
+            dma((w_dev,)), dma((w_dev,)), dma((w_dev,)), dma((w_dev,)),
+        ],
+        compiler_params=pltpu.CompilerParams(
+            collective_id=0, has_side_effects=True, vmem_limit_bytes=56 * 1024 * 1024
+        ),
+    )(traces, *factors, keep, sel)
+    scale = 1.0 / math.sqrt(w_dev * nw)
+    return (stacks * scale).reshape(n_src, r_dev, 2, f_dev)
+
+
 def solution(mesh):
     return jax.shard_map(
         body,

time: 114 us -> 60.3 us (0.53)
  Pallas kernels: 0 us -> 53.5 us
  waiting for transfers between devices: 53.4 us -> 0 us
  local copies, waits for them, and re-layouts: 21.2 us -> 0.67 us
  matrix products: 19.5 us -> 0 us
  between operations: 13.5 us -> 0.01 us
  other arithmetic: 1.54 us -> 5.98 us
  starting transfers between devices: 4.24 us -> 0 us
    pallas_call x0 -> x1, Pallas kernels: none -> 53.5 us  [body(): pl.pallas_call(functools.partial(kernel, nw, nz, w_dev, r_dev, F), out_sh...]
    psum x1 -> x0, waiting for transfers between devices: 33.3 us -> none  [body(): src = lax.psum(rows.astype(jnp.bfloat16), 'rcv')]
    all_to_all x1 -> x0, waiting for transfers between devices: 20.1 us -> none  [body(): got = lax.all_to_all(pieces, 'win', 0, 0, tiled=True)]
    dot_general x4 -> x0, matrix products: 19.5 us -> none  [the longest x1 11 us: body(): jnp.dot(traces.reshape(w_dev * r_dev, samples), table, preferred_element_...]
    dot_general x2 -> x0, local copies, waits for them, and re-layouts: 5.11 us -> none  [the longest x1 2.94 us: body(): jnp.einsum('gcwsf,gcwrf->srf', src, turned, preferred_element_type=jnp.fl...]
    all_to_all x1 -> x0, starting transfers between devices: 4.24 us -> none  [body(): got = lax.all_to_all(pieces, 'win', 0, 0, tiled=True)]
    reshape x2 -> x0, local copies, waits for them, and re-layouts: 4.23 us -> none  [the longest x1 2.98 us: body(): got = got.reshape(n_win, 2, w_dev, r_dev, f_dev)]
    mul x1 -> x0, local copies, waits for them, and re-layouts: 4.1 us -> none  [body(): return jnp.stack([real, imag], axis=2) * scale]
  transfers between devices with their start and end apart: 2 -> 0, of which waited for: 2 -> 0; matrix products, arithmetic and copies ran while one was open for 5% -> 0% of each run, Pallas kernels for 0% -> 0%
where the time goes in v2:
time: 60.3 us; the launch traced here: 60.2 us
  Pallas kernels  53.5 us (89%)
  other arithmetic  5.98 us (10%)
  local copies, waits for them, and re-layouts  0.67 us (1%)
    pallas_call x1, Pallas kernels, body(): pl.pallas_call(functools.partial(kernel, nw, nz, w_dev, r_dev, F), out_sh...  53.5 us
    mul x1, other arithmetic, body(): return (stacks * scale).reshape(n_src, r_dev, 2, f_dev)  4 us
    convert_element_type x1, other arithmetic, body(): sel = (src_station[:, None] == station_ids[None, :]).astype(jnp.bfloat16)  1.32 us

profile of v2, /device:TPU:0, one launch (start us, length us, event | category | flops | bytes accessed | tf_op | source)
XLA Modules:
  0.0 60.2 jit_solution(11722527202646888605)
XLA Ops:
  0.0 0.7 %convert_element_type.6 = f32[8]{0:T(128)S(1)} convert(s32[8]{0:T(128)} %param.8) | non-fusion elementwise | flops 8 | bytes 64 | tf_op jit(solution)/shard_map/convert_element_type | solution.py:262
  0.7 0.7 %broadcast_in_dim.2.keep = f32[8,1,128]{2,1,0:T(1,128)} broadcast(f32[8]{0:T(128)S(1)} %convert_element_type.6), dimensions={0} | broadcast | bytes 4128 | tf_op jit(solution)/shard_map/broadcast_in_dim | solution.py:262
  1.3 1.3 %compare_convert_fusion.sel = bf16[32,96]{1,0:T(8,128)(2,1)} fusion(s32[96]{0:T(128)S(1)} %iota_add_fusion, s32[32]{0:T(128)} %param.9), kind=kLoop, calls=%fused_computation.1 | loop fusion | flops 6144 | bytes 6656 | tf_op jit(solution)/shard_map/convert_element_type | solution.py:261
  2.7 53.5 %shard_map.73 = f32[32,192,128]{2,1,0:T(8,128)} custom-call(bf16[8,96,4096]{2,1,0:T(8,128)(2,1)} %traces.1, f32[64,512]{1,0:T(8,128)} %constant.16.clone.c1, f32[64,512]{1,0:T(8,128)} %constant.17.clone.s1, f32[64,512]{1,0:T(8,128)} %constant.18.clone.c0, f32[64,512]{1,0:T(8,128)} %constant.19.clone.s0, f32[8,1,128]{2,1,0:T(1,128)} %broadcast_in_dim.2.keep, ...), custom_call_target="tpu_custom_call" | custom-call | tf_op jit(solution)/shard_map/pallas_call | solution.py:268
  56.2 4.0 %broadcast_multiply_fusion = f32[32,192,128]{2,1,0:T(8,128)} fusion(f32[32,192,128]{2,1,0:T(8,128)} %shard_map.73), kind=kLoop, calls=%fused_computation | loop fusion | flops 786432 | bytes 6291456 | tf_op jit(solution)/shard_map/mul | solution.py:290
  (1 shorter events, 0.0 us)

commit v3 on v2

--- a/solution.py
+++ b/solution.py
@@ -13,6 +13,7 @@
 F = 512
 SPLIT = 64
 MM = 2
+LAG = 1
 MESH = pl.DeviceIdType.MESH
 
 
@@ -65,15 +66,21 @@
 
 def kernel(
     nw, nz, w_dev, r_dev, bins,
-    traces, c1, s1, c0, s0, keep, sel, out,
-    tr, table, spec, snd, got, own, pin, sin, pout, sout, srcf, rf,
+    traces, c1, s1, c0, s0, valid, stations, out,
+    tr, table, spec, snd, got, own, pin, sin, pout, sout, self32, srcf, rf,
     tsem, ysend, yrecv, psend, precv, ssend, srecv,
 ):
     me = lax.axis_index("win")
     z = lax.axis_index("rcv")
     f_dev = bins // nw
-    peers = [lax.rem(me + d, nw) for d in range(1, nw)]
-    senders = [lax.rem(me + nw - d, nw) for d in range(1, nw)]
+    n_src = out.shape[0]
+    half = nw // 2
+    units = w_dev // MM
+    chip = me // half
+    core = lax.rem(me, half)
+    near, far = chip * half, (1 - chip) * half
+    peers = [far + core, far + (1 - core), near + (1 - core)]
+    senders = peers
     barrier = pltpu.get_barrier_semaphore()
 
     def load(w):
@@ -108,6 +115,9 @@
         return 0
 
     lax.fori_loop(0, c1.shape[0], build, 0)
+    here = lax.broadcasted_iota(jnp.int32, (1, r_dev), 1) + z * r_dev
+    for s in range(n_src):
+        self32[s:s + 1, :] = jnp.where(here == stations[s], 1.0, 0.0).astype(jnp.float32)
     out[...] = jnp.zeros_like(out)
 
     @pl.when((z > 0) & (z < nz - 1))
@@ -132,7 +142,7 @@
             device_id={"win": peers[k]}, device_id_type=MESH,
         )
 
-    def transform(t, _):
+    def transform(t):
         for wl in range(MM):
             load(t * MM + wl).wait()
         x = tr[pl.ds(t * MM, MM)].reshape(MM * r_dev, tr.shape[2])
@@ -144,7 +154,7 @@
             rows = slice(wl * r_dev, (wl + 1) * r_dev)
             s = spec[rows, :]
             power = jnp.sum(s * s, axis=1, keepdims=True) / bins
-            gain = lax.rsqrt(power + 1e-06) * keep[w][:, 0:1]
+            gain = lax.rsqrt(power + 1e-06) * valid[w].astype(jnp.float32)
             for d in range(nw):
                 for c in range(2):
                     lo = c * bins + d * f_dev
@@ -152,101 +162,133 @@
             for k in range(nw - 1):
                 y_copy(k, w).start()
             got[me, w] = snd[me, w]
-        return 0
-
-    lax.fori_loop(0, w_dev // MM, transform, 0)
-
-    def right(j):
+
+    def unit(h, j):
+        return (0, pl.ds(j * MM, MM)) if h == 0 else (1, pl.ds(j, 1))
+
+    def sem(h, j):
+        return j if h == 0 else units + j
+
+    def right(h, j):
         return pltpu.make_async_remote_copy(
-            src_ref=pout.at[j], dst_ref=pin.at[j], send_sem=psend.at[j], recv_sem=precv.at[j],
+            src_ref=pout.at[unit(h, j)], dst_ref=pin.at[unit(h, j)],
+            send_sem=psend.at[sem(h, j)], recv_sem=precv.at[sem(h, j)],
             device_id={"rcv": lax.rem(z + 1, nz)}, device_id_type=MESH,
         )
 
-    def left(j):
+    def left(h, j):
         return pltpu.make_async_remote_copy(
-            src_ref=sout.at[j], dst_ref=sin.at[j], send_sem=ssend.at[j], recv_sem=srecv.at[j],
+            src_ref=sout.at[unit(h, j)], dst_ref=sin.at[unit(h, j)],
+            send_sem=ssend.at[sem(h, j)], recv_sem=srecv.at[sem(h, j)],
             device_id={"rcv": lax.rem(z + nz - 1, nz)}, device_id_type=MESH,
         )
 
+    def select(h, w):
+        pick = self32[...].astype(jnp.bfloat16)
+        for gl in range(half):
+            for c in range(2):
+                own[h, w, gl, c] = jnp.dot(
+                    pick, got[(near, far)[h] + gl, w, c], preferred_element_type=jnp.float32
+                ).astype(jnp.bfloat16)
+
+    def hops(h, clock, count):
+        jr = clock - z
+        jl = clock - (nz - 1 - z)
+
+        @pl.when((jr >= 0) & (jr < count))
+        def _():
+            @pl.when(z > 0)
+            def _():
+                right(h, jr).wait_recv()
+
+            @pl.when(z < nz - 1)
+            def _():
+                pout[unit(h, jr)] = own[unit(h, jr)] + pin[unit(h, jr)]
+                right(h, jr).start()
+
+        @pl.when((jl >= 0) & (jl < count))
+        def _():
+            @pl.when(z < nz - 1)
+            def _():
+                left(h, jl).wait_recv()
+
+            @pl.when(z > 0)
+            def _():
+                sout[unit(h, jl)] = own[unit(h, jl)] + sin[unit(h, jl)]
+                left(h, jl).start()
+
+    def correlate(w):
+        for h in range(2):
+            for gl in range(half):
+                i = h * half + gl
+                g = (near, far)[h] + gl
+                for c in range(2):
+                    srcf[i, c] = (
+                        own[h, w, gl, c] + pin[h, w, gl, c] + sin[h, w, gl, c]
+                    ).astype(jnp.float32)
+                re = got[g, w, 0].astype(jnp.float32)
+                im = got[g, w, 1].astype(jnp.float32)
+                rf[i, 0, pl.ds(0, r_dev, stride=2), :] = re
+                rf[i, 0, pl.ds(1, r_dev, stride=2), :] = im
+                rf[i, 1, pl.ds(0, r_dev, stride=2), :] = im
+                rf[i, 1, pl.ds(1, r_dev, stride=2), :] = -re
+
+        def accumulate(s, _):
+            total = out[s]
+            for i in range(nw):
+                total = total + srcf[i, 0, pl.ds(s, 1), :] * rf[i, 0]
+                total = total + srcf[i, 1, pl.ds(s, 1), :] * rf[i, 1]
+            out[s] = total
+            return 0
+
+        lax.fori_loop(0, n_src, accumulate, 0)
+
     def step(it, _):
-        @pl.when(it < w_dev)
-        def _():
-            for k in range(nw - 1):
-                y_arrival(k, it).wait_recv()
-            for g in range(nw):
-                for c in range(2):
-                    own[it, g, c] = jnp.dot(
-                        sel[...], got[g, it, c], preferred_element_type=jnp.float32
-                    ).astype(jnp.bfloat16)
-
-        jr = it - z
-
-        @pl.when((jr >= 0) & (jr < w_dev))
-        def _():
-            @pl.when(z > 0)
-            def _():
-                right(jr).wait_recv()
-
-            @pl.when(z < nz - 1)
-            def _():
-                pout[jr] = own[jr] + pin[jr]
-                right(jr).start()
-
-        jl = it - (nz - 1 - z)
-
-        @pl.when((jl >= 0) & (jl < w_dev))
-        def _():
-            @pl.when(z < nz - 1)
-            def _():
-                left(jl).wait_recv()
-
-            @pl.when(z > 0)
-            def _():
-                sout[jl] = own[jl] + sin[jl]
-                left(jl).start()
-
-        jc = it - (nz - 1)
-
-        @pl.when(jc >= 0)
-        def _():
-            srcf[...] = (own[jc] + pin[jc] + sin[jc]).astype(jnp.float32)
-            for g in range(nw):
-                re = got[g, jc, 0].astype(jnp.float32)
-                im = got[g, jc, 1].astype(jnp.float32)
-                rf[g, 0, pl.ds(0, r_dev, stride=2), :] = re
-                rf[g, 0, pl.ds(1, r_dev, stride=2), :] = im
-                rf[g, 1, pl.ds(0, r_dev, stride=2), :] = im
-                rf[g, 1, pl.ds(1, r_dev, stride=2), :] = -re
-
-            def accumulate(s, _):
-                total = out[s]
-                for g in range(nw):
-                    total = total + srcf[g, 0, pl.ds(s, 1), :] * rf[g, 0]
-                    total = total + srcf[g, 1, pl.ds(s, 1), :] * rf[g, 1]
-                out[s] = total
-                return 0
-
-            lax.fori_loop(0, out.shape[0], accumulate, 0)
+        @pl.when(it < units)
+        def _():
+            transform(it)
+            for wl in range(MM):
+                y_arrival(2, it * MM + wl).wait_recv()
+                select(0, it * MM + wl)
+
+        hops(0, it, units)
+
+        @pl.when((it >= LAG) & (it < w_dev + LAG))
+        def _():
+            y_arrival(0, it - LAG).wait_recv()
+            y_arrival(1, it - LAG).wait_recv()
+            select(1, it - LAG)
+
+        hops(1, it - LAG, w_dev)
+
+        @pl.when(it >= LAG + nz - 1)
+        def _():
+            correlate(it - LAG - (nz - 1))
 
         return 0
 
-    lax.fori_loop(0, w_dev + nz - 1, step, 0)
+    lax.fori_loop(0, w_dev + LAG + nz - 1, step, 0)
 
     def drain(w, _):
         for k in range(nw - 1):
             y_copy(k, w).wait_send()
-
-        @pl.when(z < nz - 1)
-        def _():
-            right(w).wait_send()
-
-        @pl.when(z > 0)
-        def _():
-            left(w).wait_send()
-
         return 0
 
     lax.fori_loop(0, w_dev, drain, 0)
+
+    for h, count in ((0, units), (1, w_dev)):
+        def drain_chain(j, _, h=h):
+            @pl.when(z < nz - 1)
+            def _():
+                right(h, j).wait_send()
+
+            @pl.when(z > 0)
+            def _():
+                left(h, j).wait_send()
+
+            return 0
+
+        lax.fori_loop(0, count, drain_chain, 0)
 
 
 def body(traces, valid, src_station):
@@ -254,21 +296,20 @@
     nw, nz = lax.axis_size("win"), lax.axis_size("rcv")
     f_dev = F // nw
     n_src = src_station.shape[0]
-    if f_dev % 128 or r_dev % 16 or w_dev % MM:
+    if nw != 4 or f_dev % 128 or r_dev % 16 or w_dev % MM:
         return plain_body(traces, valid, src_station)
     factors = [jnp.asarray(f) for f in angle_factors(samples, F, samples // 16)]
-    station_ids = lax.axis_index("rcv") * r_dev + jnp.arange(r_dev, dtype=jnp.int32)
-    sel = (src_station[:, None] == station_ids[None, :]).astype(jnp.bfloat16)
-    keep = jnp.broadcast_to(valid.astype(jnp.float32)[:, None, None], (w_dev, 1, 128))
     vmem = pl.BlockSpec(memory_space=pltpu.VMEM)
     bf16, f32 = jnp.bfloat16, jnp.float32
     spectra = (nw, w_dev, 2, r_dev, f_dev)
-    rows = (w_dev, nw, 2, n_src, f_dev)
+    rows = (2, w_dev, nw // 2, 2, n_src, f_dev)
+    chain = (w_dev // MM + w_dev,)
+    smem = pl.BlockSpec(memory_space=pltpu.SMEM)
     dma = pltpu.SemaphoreType.DMA
     stacks = pl.pallas_call(
         functools.partial(kernel, nw, nz, w_dev, r_dev, F),
         out_shape=jax.ShapeDtypeStruct((n_src, 2 * r_dev, f_dev), f32),
-        in_specs=[pl.BlockSpec(memory_space=pl.ANY)] + [vmem] * 6,
+        in_specs=[pl.BlockSpec(memory_space=pltpu.HBM)] + [vmem] * 4 + [smem] * 2,
         out_specs=vmem,
         scratch_shapes=[
             pltpu.VMEM((w_dev, r_dev, samples), bf16),
@@ -277,15 +318,16 @@
             pltpu.VMEM(spectra, bf16),
             pltpu.VMEM(spectra, bf16),
         ] + [pltpu.VMEM(rows, bf16)] * 5 + [
+            pltpu.VMEM((n_src, r_dev), f32),
             pltpu.VMEM((nw, 2, n_src, f_dev), f32),
             pltpu.VMEM((nw, 2, 2 * r_dev, f_dev), f32),
             dma((w_dev,)), dma((nw - 1, w_dev)), dma((nw - 1, w_dev)),
-            dma((w_dev,)), dma((w_dev,)), dma((w_dev,)), dma((w_dev,)),
+            dma(chain), dma(chain), dma(chain), dma(chain),
         ],
         compiler_params=pltpu.CompilerParams(
-            collective_id=0, has_side_effects=True, vmem_limit_bytes=56 * 1024 * 1024
+            collective_id=0, has_side_effects=True, vmem_limit_bytes=32 * 1024 * 1024
         ),
-    )(traces, *factors, keep, sel)
+    )(traces, *factors, valid, src_station)
     scale = 1.0 / math.sqrt(w_dev * nw)
     return (stacks * scale).reshape(n_src, r_dev, 2, f_dev)
 

time: 60.3 us -> 59.2 us (0.982)
  local copies, waits for them, and re-layouts: 0.67 us -> 7.71 us
  Pallas kernels: 53.5 us -> 49.3 us
  other arithmetic: 5.98 us -> 1.94 us
    unnamed x0 -> x14, local copies, waits for them, and re-layouts: none -> 7.71 us
    pallas_call x1, Pallas kernels: 53.5 us -> 49.3 us  [body(): pl.pallas_call(functools.partial(kernel, nw, nz, w_dev, r_dev, F), out_sh...]
    mul x1, other arithmetic: 4 us -> 1.94 us  [body(): return (stacks * scale).reshape(n_src, r_dev, 2, f_dev)]
    convert_element_type x2 -> x0, other arithmetic: 1.98 us -> none  [the longest x1 1.32 us: body(): sel = (src_station[:, None] == station_ids[None, :]).astype(jnp.bfloat16)]
    broadcast_in_dim x1 -> x0, local copies, waits for them, and re-layouts: 0.67 us -> none  [body(): jnp.broadcast_to(valid.astype(jnp.float32)[:, None, None], (w_dev, 1, 128))]
where the time goes in v3:
time: 59.2 us; the launch traced here: 59 us
  Pallas kernels  49.3 us (83%)
  local copies, waits for them, and re-layouts  7.71 us (13%)
  other arithmetic  1.94 us (3%)
    pallas_call x1, Pallas kernels, body(): pl.pallas_call(functools.partial(kernel, nw, nz, w_dev, r_dev, F), out_sh...  49.3 us
    unnamed x14, local copies, waits for them, and re-layouts  7.71 us
    mul x1, other arithmetic, body(): return (stacks * scale).reshape(n_src, r_dev, 2, f_dev)  1.94 us

profile of v3, /device:TPU:0, one launch (start us, length us, event | category | flops | bytes accessed | tf_op | source)
XLA Modules:
  0.0 59.0 jit_solution(4558641183130706250)
XLA Ops:
  0.0 0.0 copy-start
  0.0 2.8 %copy-done = bf16[8,96,4096]{2,1,0:T(8,128)(2,1)S(1)} copy-done((bf16[8,96,4096]{2,1,0:T(8,128)(2,1)S(1)}, bf16[8,96,4096]{2,1,0:T(8,128)(2,1)}, u32[]{:S(2)}) %copy-start) | copy-done | bytes 6291480
  2.8 0.0 copy-start.1
  2.8 0.9 %copy-done.1 = f32[64,512]{1,0:T(8,128)S(1)} copy-done((f32[64,512]{1,0:T(8,128)S(1)}, f32[64,512]{1,0:T(8,128)}, u32[]{:S(2)}) %copy-start.1) | copy-done | bytes 131096
  3.7 0.0 copy-start.2
  3.7 0.9 %copy-done.2 = f32[64,512]{1,0:T(8,128)S(1)} copy-done((f32[64,512]{1,0:T(8,128)S(1)}, f32[64,512]{1,0:T(8,128)}, u32[]{:S(2)}) %copy-start.2) | copy-done | bytes 131096
  4.6 0.0 copy-start.3
  4.6 0.9 %copy-done.3 = f32[64,512]{1,0:T(8,128)S(1)} copy-done((f32[64,512]{1,0:T(8,128)S(1)}, f32[64,512]{1,0:T(8,128)}, u32[]{:S(2)}) %copy-start.3) | copy-done | bytes 131096
  5.5 0.0 copy-start.4
  5.5 0.9 %copy-done.4 = f32[64,512]{1,0:T(8,128)S(1)} copy-done((f32[64,512]{1,0:T(8,128)S(1)}, f32[64,512]{1,0:T(8,128)}, u32[]{:S(2)}) %copy-start.4) | copy-done | bytes 131096
  6.4 0.0 copy-start.5
  6.4 0.7 %copy-done.5 = s32[8]{0:T(128)S(1)} copy-done((s32[8]{0:T(128)S(1)}, s32[8]{0:T(128)}, u32[]{:S(2)}) %copy-start.5) | copy-done | bytes 56
  7.1 0.0 copy-start.6
  7.1 0.7 %copy-done.6 = s32[32]{0:T(128)S(1)} copy-done((s32[32]{0:T(128)S(1)}, s32[32]{0:T(128)}, u32[]{:S(2)}) %copy-start.6) | copy-done | bytes 152
  7.7 49.3 %shard_map.73 = f32[32,192,128]{2,1,0:T(8,128)S(1)} custom-call(bf16[8,96,4096]{2,1,0:T(8,128)(2,1)S(1)} %copy-done, f32[64,512]{1,0:T(8,128)S(1)} %copy-done.4, f32[64,512]{1,0:T(8,128)S(1)} %copy-done.3, f32[64,512]{1,0:T(8,128)S(1)} %copy-done.2, f32[64,512]{1,0:T(8,128)S(1)} %copy-done.1, s32[8]{0:T(128)S(1)} %copy-done.5, s32[32]{0:T(128)S(1)} %copy-done.6), custom_call_target="tpu_custom_call" | custom-call | tf_op jit(solution)/shard_map/pallas_call | solution.py:309
  57.0 1.9 %broadcast_multiply_fusion = f32[32,192,128]{2,1,0:T(8,128)} fusion(f32[32,192,128]{2,1,0:T(8,128)S(1)} %shard_map.73), kind=kLoop, calls=%fused_computation | loop fusion | flops 786432 | bytes 6291456 | tf_op jit(solution)/shard_map/mul | solution.py:332
Async XLA Ops:
  0.0 2.8 %copy-start = (bf16[8,96,4096]{2,1,0:T(8,128)(2,1)S(1)}, bf16[8,96,4096]{2,1,0:T(8,128)(2,1)}, u32[]{:S(2)}) copy-start(bf16[8,96,4096]{2,1,0:T(8,128)(2,1)} %traces.1) | copy-start | bytes 18874372
  2.8 0.9 %copy-start.1 = (f32[64,512]{1,0:T(8,128)S(1)}, f32[64,512]{1,0:T(8,128)}, u32[]{:S(2)}) copy-start(f32[64,512]{1,0:T(8,128)} %constant.13.clone.s0) | copy-start | bytes 393220
  3.7 0.9 %copy-start.2 = (f32[64,512]{1,0:T(8,128)S(1)}, f32[64,512]{1,0:T(8,128)}, u32[]{:S(2)}) copy-start(f32[64,512]{1,0:T(8,128)} %constant.12.clone.c0) | copy-start | bytes 393220
  4.6 0.9 %copy-start.3 = (f32[64,512]{1,0:T(8,128)S(1)}, f32[64,512]{1,0:T(8,128)}, u32[]{:S(2)}) copy-start(f32[64,512]{1,0:T(8,128)} %constant.11.clone.s1) | copy-start | bytes 393220
  5.5 0.9 %copy-start.4 = (f32[64,512]{1,0:T(8,128)S(1)}, f32[64,512]{1,0:T(8,128)}, u32[]{:S(2)}) copy-start(f32[64,512]{1,0:T(8,128)} %constant.10.clone.c1) | copy-start | bytes 393220
  6.4 0.7 %copy-start.5 = (s32[8]{0:T(128)S(1)}, s32[8]{0:T(128)}, u32[]{:S(2)}) copy-start(s32[8]{0:T(128)} %valid.1) | copy-start | bytes 100
  7.1 0.7 %copy-start.6 = (s32[32]{0:T(128)S(1)}, s32[32]{0:T(128)}, u32[]{:S(2)}) copy-start(s32[32]{0:T(128)} %stations.1) | copy-start | bytes 388

commit v4 on v3

--- a/solution.py
+++ b/solution.py
@@ -14,6 +14,8 @@
 SPLIT = 64
 MM = 2
 LAG = 1
+HOP = 2
+GRANT = 48
 MESH = pl.DeviceIdType.MESH
 
 
@@ -66,7 +68,7 @@
 
 def kernel(
     nw, nz, w_dev, r_dev, bins,
-    traces, c1, s1, c0, s0, valid, stations, out,
+    traces, factors, valid, stations, out,
     tr, table, spec, snd, got, own, pin, sin, pout, sout, self32, srcf, rf,
     tsem, ysend, yrecv, psend, precv, ssend, srecv,
 ):
@@ -107,14 +109,19 @@
     def _():
         sin[...] = jnp.zeros_like(sin)
 
+    coarse = tr.shape[2] // SPLIT
+    fine = slice(2 * coarse, 2 * coarse + SPLIT)
+    fine_sin = slice(2 * coarse + SPLIT, 2 * coarse + 2 * SPLIT)
+
     def build(a, _):
-        ca, sa = c1[pl.ds(a, 1), :], s1[pl.ds(a, 1), :]
+        ca, sa = factors[pl.ds(a, 1), :], factors[pl.ds(coarse + a, 1), :]
+        c0, s0 = factors[fine, :], factors[fine_sin, :]
         rows = pl.ds(pl.multiple_of(a * SPLIT, SPLIT), SPLIT)
-        table[rows, 0:bins] = (ca * c0[...] - sa * s0[...]).astype(jnp.bfloat16)
-        table[rows, bins:] = (-(sa * c0[...] + ca * s0[...])).astype(jnp.bfloat16)
+        table[rows, 0:bins] = (ca * c0 - sa * s0).astype(jnp.bfloat16)
+        table[rows, bins:] = (-(sa * c0 + ca * s0)).astype(jnp.bfloat16)
         return 0
 
-    lax.fori_loop(0, c1.shape[0], build, 0)
+    lax.fori_loop(0, coarse, build, 0)
     here = lax.broadcasted_iota(jnp.int32, (1, r_dev), 1) + z * r_dev
     for s in range(n_src):
         self32[s:s + 1, :] = jnp.where(here == stations[s], 1.0, 0.0).astype(jnp.float32)
@@ -192,8 +199,8 @@
                 ).astype(jnp.bfloat16)
 
     def hops(h, clock, count):
-        jr = clock - z
-        jl = clock - (nz - 1 - z)
+        jr = clock - HOP * z
+        jl = clock - HOP * (nz - 1 - z)
 
         @pl.when((jr >= 0) & (jr < count))
         def _():
@@ -233,15 +240,22 @@
                 rf[i, 1, pl.ds(0, r_dev, stride=2), :] = im
                 rf[i, 1, pl.ds(1, r_dev, stride=2), :] = -re
 
-        def accumulate(s, _):
-            total = out[s]
-            for i in range(nw):
-                total = total + srcf[i, 0, pl.ds(s, 1), :] * rf[i, 0]
-                total = total + srcf[i, 1, pl.ds(s, 1), :] * rf[i, 1]
-            out[s] = total
+        def accumulate(q, _):
+            for lo in range(0, 2 * r_dev, r_dev):
+                rows = slice(lo, lo + r_dev)
+                totals = [out[q * 4 + u, rows, :] for u in range(4)]
+                for i in range(nw):
+                    for c in range(2):
+                        other = rf[i, c, rows, :]
+                        totals = [
+                            total + srcf[i, c, pl.ds(q * 4 + u, 1), :] * other
+                            for u, total in enumerate(totals)
+                        ]
+                for u in range(4):
+                    out[q * 4 + u, rows, :] = totals[u]
             return 0
 
-        lax.fori_loop(0, n_src, accumulate, 0)
+        lax.fori_loop(0, n_src // 4, accumulate, 0)
 
     def step(it, _):
         @pl.when(it < units)
@@ -261,13 +275,13 @@
 
         hops(1, it - LAG, w_dev)
 
-        @pl.when(it >= LAG + nz - 1)
-        def _():
-            correlate(it - LAG - (nz - 1))
+        @pl.when(it >= LAG + HOP * (nz - 1))
+        def _():
+            correlate(it - LAG - HOP * (nz - 1))
 
         return 0
 
-    lax.fori_loop(0, w_dev + LAG + nz - 1, step, 0)
+    lax.fori_loop(0, w_dev + LAG + HOP * (nz - 1), step, 0)
 
     def drain(w, _):
         for k in range(nw - 1):
@@ -296,9 +310,9 @@
     nw, nz = lax.axis_size("win"), lax.axis_size("rcv")
     f_dev = F // nw
     n_src = src_station.shape[0]
-    if nw != 4 or f_dev % 128 or r_dev % 16 or w_dev % MM:
+    if nw != 4 or f_dev % 128 or r_dev % 16 or w_dev % MM or n_src % 4:
         return plain_body(traces, valid, src_station)
-    factors = [jnp.asarray(f) for f in angle_factors(samples, F, samples // 16)]
+    factors = jnp.asarray(np.concatenate(angle_factors(samples, F, samples // 16)))
     vmem = pl.BlockSpec(memory_space=pltpu.VMEM)
     bf16, f32 = jnp.bfloat16, jnp.float32
     spectra = (nw, w_dev, 2, r_dev, f_dev)
@@ -309,7 +323,7 @@
     stacks = pl.pallas_call(
         functools.partial(kernel, nw, nz, w_dev, r_dev, F),
         out_shape=jax.ShapeDtypeStruct((n_src, 2 * r_dev, f_dev), f32),
-        in_specs=[pl.BlockSpec(memory_space=pltpu.HBM)] + [vmem] * 4 + [smem] * 2,
+        in_specs=[pl.BlockSpec(memory_space=pltpu.HBM)] + [vmem] + [smem] * 2,
         out_specs=vmem,
         scratch_shapes=[
             pltpu.VMEM((w_dev, r_dev, samples), bf16),
@@ -325,9 +339,9 @@
             dma(chain), dma(chain), dma(chain), dma(chain),
         ],
         compiler_params=pltpu.CompilerParams(
-            collective_id=0, has_side_effects=True, vmem_limit_bytes=32 * 1024 * 1024
+            collective_id=0, has_side_effects=True, vmem_limit_bytes=GRANT * 1024 * 1024
         ),
-    )(traces, *factors, valid, src_station)
+    )(traces, factors, valid, src_station)
     scale = 1.0 / math.sqrt(w_dev * nw)
     return (stacks * scale).reshape(n_src, r_dev, 2, f_dev)
 

time: 59.2 us -> 49.9 us (0.84)
  local copies, waits for them, and re-layouts: 7.71 us -> 2.35 us
  Pallas kernels: 49.3 us -> 45.4 us
    unnamed x14 -> x6, local copies, waits for them, and re-layouts: 7.71 us -> 2.35 us
    pallas_call x1, Pallas kernels: 49.3 us -> 45.4 us  [body(): pl.pallas_call(functools.partial(kernel, nw, nz, w_dev, r_dev, F), out_sh...]
where the time goes in v4:
time: 49.9 us; the launch traced here: 49.7 us
  Pallas kernels  45.4 us (91%)
  local copies, waits for them, and re-layouts  2.35 us (5%)
  other arithmetic  1.94 us (4%)
    pallas_call x1, Pallas kernels, body(): pl.pallas_call(functools.partial(kernel, nw, nz, w_dev, r_dev, F), out_sh...  45.4 us
    unnamed x6, local copies, waits for them, and re-layouts  2.35 us
    mul x1, other arithmetic, body(): return (stacks * scale).reshape(n_src, r_dev, 2, f_dev)  1.94 us

profile of v4, /device:TPU:0, one launch (start us, length us, event | category | flops | bytes accessed | tf_op | source)
XLA Modules:
  0.0 49.7 jit_solution(13688240876050382281)
XLA Ops:
  0.0 0.0 copy-start
  0.0 1.0 %copy-done = f32[256,512]{1,0:T(8,128)S(1)} copy-done((f32[256,512]{1,0:T(8,128)S(1)}, f32[256,512]{1,0:T(8,128)}, u32[]{:S(2)}) %copy-start) | copy-done | bytes 524312
  1.0 0.0 copy-start.1
  1.0 0.7 %copy-done.1 = s32[8]{0:T(128)S(1)} copy-done((s32[8]{0:T(128)S(1)}, s32[8]{0:T(128)}, u32[]{:S(2)}) %copy-start.1) | copy-done | bytes 56
  1.7 0.0 copy-start.2
  1.7 0.7 %copy-done.2 = s32[32]{0:T(128)S(1)} copy-done((s32[32]{0:T(128)S(1)}, s32[32]{0:T(128)}, u32[]{:S(2)}) %copy-start.2) | copy-done | bytes 152
  2.4 45.4 %shard_map.46 = f32[32,192,128]{2,1,0:T(8,128)S(1)} custom-call(bf16[8,96,4096]{2,1,0:T(8,128)(2,1)} %traces.1, f32[256,512]{1,0:T(8,128)S(1)} %copy-done, s32[8]{0:T(128)S(1)} %copy-done.1, s32[32]{0:T(128)S(1)} %copy-done.2), custom_call_target="tpu_custom_call" | custom-call | tf_op jit(solution)/shard_map/pallas_call | solution.py:323
  47.8 1.9 %broadcast_multiply_fusion = f32[32,192,128]{2,1,0:T(8,128)} fusion(f32[32,192,128]{2,1,0:T(8,128)S(1)} %shard_map.46), kind=kLoop, calls=%fused_computation | loop fusion | flops 786432 | bytes 6291456 | tf_op jit(solution)/shard_map/mul | solution.py:346
Async XLA Ops:
  0.0 1.0 %copy-start = (f32[256,512]{1,0:T(8,128)S(1)}, f32[256,512]{1,0:T(8,128)}, u32[]{:S(2)}) copy-start(f32[256,512]{1,0:T(8,128)} %constant.4.clone.factors) | copy-start | bytes 1572868
  1.0 0.7 %copy-start.1 = (s32[8]{0:T(128)S(1)}, s32[8]{0:T(128)}, u32[]{:S(2)}) copy-start(s32[8]{0:T(128)} %valid.1) | copy-start | bytes 100
  1.7 0.7 %copy-start.2 = (s32[32]{0:T(128)S(1)}, s32[32]{0:T(128)}, u32[]{:S(2)}) copy-start(s32[32]{0:T(128)} %stations.1) | copy-start | bytes 388

commit v5 on v4

--- a/solution.py
+++ b/solution.py
@@ -14,7 +14,7 @@
 SPLIT = 64
 MM = 2
 LAG = 1
-HOP = 2
+HOP = (1, 2)
 GRANT = 48
 MESH = pl.DeviceIdType.MESH
 
@@ -199,8 +199,8 @@
                 ).astype(jnp.bfloat16)
 
     def hops(h, clock, count):
-        jr = clock - HOP * z
-        jl = clock - HOP * (nz - 1 - z)
+        jr = clock - HOP[h] * z
+        jl = clock - HOP[h] * (nz - 1 - z)
 
         @pl.when((jr >= 0) & (jr < count))
         def _():
@@ -224,27 +224,25 @@
                 sout[unit(h, jl)] = own[unit(h, jl)] + sin[unit(h, jl)]
                 left(h, jl).start()
 
-    def correlate(w):
-        for h in range(2):
-            for gl in range(half):
-                i = h * half + gl
-                g = (near, far)[h] + gl
-                for c in range(2):
-                    srcf[i, c] = (
-                        own[h, w, gl, c] + pin[h, w, gl, c] + sin[h, w, gl, c]
-                    ).astype(jnp.float32)
-                re = got[g, w, 0].astype(jnp.float32)
-                im = got[g, w, 1].astype(jnp.float32)
-                rf[i, 0, pl.ds(0, r_dev, stride=2), :] = re
-                rf[i, 0, pl.ds(1, r_dev, stride=2), :] = im
-                rf[i, 1, pl.ds(0, r_dev, stride=2), :] = im
-                rf[i, 1, pl.ds(1, r_dev, stride=2), :] = -re
+    def correlate(h, w):
+        for gl in range(half):
+            i, g = gl, (near, far)[h] + gl
+            for c in range(2):
+                srcf[i, c] = (
+                    own[h, w, gl, c] + pin[h, w, gl, c] + sin[h, w, gl, c]
+                ).astype(jnp.float32)
+            re = got[g, w, 0].astype(jnp.float32)
+            im = got[g, w, 1].astype(jnp.float32)
+            rf[i, 0, pl.ds(0, r_dev, stride=2), :] = re
+            rf[i, 0, pl.ds(1, r_dev, stride=2), :] = im
+            rf[i, 1, pl.ds(0, r_dev, stride=2), :] = im
+            rf[i, 1, pl.ds(1, r_dev, stride=2), :] = -re
 
         def accumulate(q, _):
             for lo in range(0, 2 * r_dev, r_dev):
                 rows = slice(lo, lo + r_dev)
                 totals = [out[q * 4 + u, rows, :] for u in range(4)]
-                for i in range(nw):
+                for i in range(half):
                     for c in range(2):
                         other = rf[i, c, rows, :]
                         totals = [
@@ -275,13 +273,22 @@
 
         hops(1, it - LAG, w_dev)
 
-        @pl.when(it >= LAG + HOP * (nz - 1))
-        def _():
-            correlate(it - LAG - HOP * (nz - 1))
+        near_unit = it - HOP[0] * (nz - 1)
+
+        @pl.when((near_unit >= 0) & (near_unit < units))
+        def _():
+            for wl in range(MM):
+                correlate(0, near_unit * MM + wl)
+
+        far_window = it - LAG - HOP[1] * (nz - 1)
+
+        @pl.when(far_window >= 0)
+        def _():
+            correlate(1, far_window)
 
         return 0
 
-    lax.fori_loop(0, w_dev + LAG + HOP * (nz - 1), step, 0)
+    lax.fori_loop(0, w_dev + LAG + HOP[1] * (nz - 1), step, 0)
 
     def drain(w, _):
         for k in range(nw - 1):
@@ -333,8 +340,8 @@
             pltpu.VMEM(spectra, bf16),
         ] + [pltpu.VMEM(rows, bf16)] * 5 + [
             pltpu.VMEM((n_src, r_dev), f32),
-            pltpu.VMEM((nw, 2, n_src, f_dev), f32),
-            pltpu.VMEM((nw, 2, 2 * r_dev, f_dev), f32),
+            pltpu.VMEM((nw // 2, 2, n_src, f_dev), f32),
+            pltpu.VMEM((nw // 2, 2, 2 * r_dev, f_dev), f32),
             dma((w_dev,)), dma((nw - 1, w_dev)), dma((nw - 1, w_dev)),
             dma(chain), dma(chain), dma(chain), dma(chain),
         ],

time: 49.9 us -> 49.5 us (level)
  no operation moved by 1% of the time
where the time goes in v5:
time: 49.5 us; the launch traced here: 49.3 us
  Pallas kernels  45 us (91%)
  local copies, waits for them, and re-layouts  2.35 us (5%)
  other arithmetic  1.94 us (4%)
    pallas_call x1, Pallas kernels, body(): pl.pallas_call(functools.partial(kernel, nw, nz, w_dev, r_dev, F), out_sh...  45 us
    unnamed x6, local copies, waits for them, and re-layouts  2.35 us
    mul x1, other arithmetic, body(): return (stacks * scale).reshape(n_src, r_dev, 2, f_dev)  1.94 us

profile of v5, /device:TPU:0, one launch (start us, length us, event | category | flops | bytes accessed | tf_op | source)
XLA Modules:
  0.0 49.3 jit_solution(14680883671183778383)
XLA Ops:
  0.0 0.0 copy-start
  0.0 1.0 %copy-done = f32[256,512]{1,0:T(8,128)S(1)} copy-done((f32[256,512]{1,0:T(8,128)S(1)}, f32[256,512]{1,0:T(8,128)}, u32[]{:S(2)}) %copy-start) | copy-done | bytes 524312
  1.0 0.0 copy-start.1
  1.0 0.7 %copy-done.1 = s32[8]{0:T(128)S(1)} copy-done((s32[8]{0:T(128)S(1)}, s32[8]{0:T(128)}, u32[]{:S(2)}) %copy-start.1) | copy-done | bytes 56
  1.7 0.0 copy-start.2
  1.7 0.7 %copy-done.2 = s32[32]{0:T(128)S(1)} copy-done((s32[32]{0:T(128)S(1)}, s32[32]{0:T(128)}, u32[]{:S(2)}) %copy-start.2) | copy-done | bytes 152
  2.4 45.0 %shard_map.46 = f32[32,192,128]{2,1,0:T(8,128)S(1)} custom-call(bf16[8,96,4096]{2,1,0:T(8,128)(2,1)} %traces.1, f32[256,512]{1,0:T(8,128)S(1)} %copy-done, s32[8]{0:T(128)S(1)} %copy-done.1, s32[32]{0:T(128)S(1)} %copy-done.2), custom_call_target="tpu_custom_call" | custom-call | tf_op jit(solution)/shard_map/pallas_call | solution.py:330
  47.3 1.9 %broadcast_multiply_fusion = f32[32,192,128]{2,1,0:T(8,128)} fusion(f32[32,192,128]{2,1,0:T(8,128)S(1)} %shard_map.46), kind=kLoop, calls=%fused_computation | loop fusion | flops 786432 | bytes 6291456 | tf_op jit(solution)/shard_map/mul | solution.py:353
Async XLA Ops:
  0.0 1.0 %copy-start = (f32[256,512]{1,0:T(8,128)S(1)}, f32[256,512]{1,0:T(8,128)}, u32[]{:S(2)}) copy-start(f32[256,512]{1,0:T(8,128)} %constant.4.clone.factors) | copy-start | bytes 1572868
  1.0 0.7 %copy-start.1 = (s32[8]{0:T(128)S(1)}, s32[8]{0:T(128)}, u32[]{:S(2)}) copy-start(s32[8]{0:T(128)} %valid.1) | copy-start | bytes 100
  1.7 0.7 %copy-start.2 = (s32[32]{0:T(128)S(1)}, s32[32]{0:T(128)}, u32[]{:S(2)}) copy-start(s32[32]{0:T(128)} %stations.1) | copy-start | bytes 388
